TPU v7x, 32 devices: a whole 2x2x4 slice. The times are simulated.
32 devices in a mesh: dp: 8 (over z, x), tensor: 4 (over y, core).
Axes of the slice: x: 2, y: 2, z: 4, core: 2. Of those that a mesh axis runs over, the one named last changes fastest.
Arguments:
- layer_input: bfloat16 [8192, 512], P(('dp', 'tensor')), may hold values from -6 to 6
- segments: int32 [8, 1024], P('dp'), may hold values from 0 to 3, never falling along the last dimension, each value on 1 to 800 neighbouring positions
- norm1_gain: bfloat16 [512], replicated, may hold values from 0.5 to 1.5
- norm1_bias: bfloat16 [512], replicated, may hold values from -4 to 4
- w_query: bfloat16 [512, 512], P(None, 'tensor'), may hold values from -0.25 to 0.25
- b_query: bfloat16 [512], P('tensor'), may hold values from -6 to 6
- w_key: bfloat16 [512, 512], P(None, 'tensor'), may hold values from -0.25 to 0.25
- w_value: bfloat16 [512, 512], P(None, 'tensor'), may hold values from -0.25 to 0.25
- b_value: bfloat16 [512], P('tensor'), may hold values from -6 to 6
- w_out: bfloat16 [512, 512], P('tensor'), may hold values from -2 to 2
- b_out: bfloat16 [512], replicated, may hold values from -4 to 4
- gate1_w: bfloat16 [512, 512], P('tensor'), may hold values from -0.25 to 0.25
- gate1_b: bfloat16 [512], replicated, may hold values from -6 to 6
- norm2_gain: bfloat16 [512], replicated, may hold values from 0.5 to 1.5
- norm2_bias: bfloat16 [512], replicated, may hold values from -4 to 4
- w_in: bfloat16 [512, 2048], P(None, 'tensor'), may hold values from -0.25 to 0.25
- b_in: bfloat16 [2048], P('tensor'), may hold values from -6 to 6
- w_back: bfloat16 [2048, 512], P('tensor'), may hold values from -0.1875 to 0.1875
- b_back: bfloat16 [512], replicated, may hold values from -4 to 4
- gate2_w: bfloat16 [512, 512], P('tensor'), may hold values from -0.25 to 0.25
- gate2_b: bfloat16 [512], replicated, may hold values from -6 to 6
- cotangent: bfloat16 [8192, 512], P(('dp', 'tensor')), may hold values from -6 to 6
Outputs:
- output: bfloat16 [8192, 512], P(('dp', 'tensor'))
- input_grad: float32 [8192, 512], P(('dp', 'tensor'))
- grad_norm1_gain: float32 [512], replicated
- grad_norm1_bias: float32 [512], replicated
- grad_w_query: float32 [512, 512], P(None, 'tensor')
- grad_b_query: float32 [512], P('tensor')
- grad_w_key: float32 [512, 512], P(None, 'tensor')
- grad_w_value: float32 [512, 512], P(None, 'tensor')
- grad_b_value: float32 [512], P('tensor')
- grad_w_out: float32 [512, 512], P('tensor')
- grad_b_out: float32 [512], replicated
- grad_gate1_w: float32 [512, 512], P('tensor')
- grad_gate1_b: float32 [512], replicated
- grad_norm2_gain: float32 [512], replicated
- grad_norm2_bias: float32 [512], replicated
- grad_w_in: float32 [512, 2048], P(None, 'tensor')
- grad_b_in: float32 [2048], P('tensor')
- grad_w_back: float32 [2048, 512], P('tensor')
- grad_b_back: float32 [512], replicated
- grad_gate2_w: float32 [512, 512], P('tensor')
- grad_gate2_b: float32 [512], replicated
Inputs may be any that keep to these rules, and one draw needn't show every extreme that they name: `segments`: document numbers never fall along a sequence; every sequence holds 4 documents, none longer than 800 tokens, and one document reaches that length.
All inputs are finite; a program needn't handle non-finite values.
Results may differ from a plain program's by a relative error of at most 0.014.
Values may be sent and summed in bfloat16 or wider, within the bound.
No kernel may reach another device: no remote copies, remote signals or barrier semaphores. Data moves between devices by JAX's collectives and lax.ppermute only.
A program may use at most 64 MiB of HBM per device.

v0:
```python
import jax
import jax.numpy as jnp
from jax import lax
from jax.sharding import PartitionSpec as P

HD = 64
EPSILON = 1e-05


def matmul(left, right):
    return jnp.dot(left, right, preferred_element_type=jnp.float32)


def inner_left(left, right):
    return lax.dot_general(
        left, right, (((0,), (0,)), ((), ())), preferred_element_type=jnp.float32
    )


def outer_right(left, right):
    return lax.dot_general(
        left, right, (((1,), (1,)), ((), ())), preferred_element_type=jnp.float32
    )


def column_sum(matrix):
    return jnp.sum(matrix, axis=0, dtype=jnp.float32)


def place_columns(full, piece, start):
    current = lax.dynamic_slice_in_dim(full, start, piece.shape[1], 1)
    return lax.dynamic_update_slice_in_dim(full, current + piece, start, 1)


def smooth_unit(values):
    return jax.nn.gelu(values, approximate=True)


def norm_forward(values, gain, shift):
    centred = values - jnp.mean(values, axis=-1, keepdims=True)
    spread = jnp.mean(centred * centred, axis=-1, keepdims=True)
    inverse = lax.rsqrt(spread + EPSILON)
    unit = centred * inverse
    return (unit * gain + shift, unit, inverse)


def norm_backward(share_grad, unit, inverse, gain):
    scaled = share_grad * gain
    grad_gain = jnp.sum(share_grad * unit, axis=0)
    grad_shift = jnp.sum(share_grad, axis=0)
    average = jnp.mean(scaled, axis=-1, keepdims=True)
    project = jnp.mean(scaled * unit, axis=-1, keepdims=True)
    return (inverse * (scaled - average - unit * project), grad_gain, grad_shift)


def head_major(matrix):
    return matrix.reshape(matrix.shape[0], -1, HD).transpose(1, 0, 2)


def row_major(heads_array):
    return heads_array.transpose(1, 0, 2).reshape(heads_array.shape[1], -1)


def split_blocks(heads_array, count, block):
    return heads_array.reshape(heads_array.shape[0], count, block, HD).transpose(1, 0, 2, 3)


def join_blocks(blocks):
    count, heads, block, width = blocks.shape
    return blocks.transpose(0, 2, 1, 3).reshape(count * block, heads * width)


def build_mask(segment_row):
    places = lax.iota(jnp.int32, segment_row.shape[0])
    same_doc = segment_row[:, None] == segment_row[None, :]
    return same_doc & (places[None, :] <= places[:, None])


def attention_forward(query, keys, values, allowed):
    rows = query.shape[0]
    block = min(512, rows)
    count = rows // block
    scale_factor = HD ** (-0.5)
    heads_k = head_major(keys)
    heads_v = head_major(values)
    query_blocks = split_blocks(head_major(query), count, block)
    mask_blocks = allowed.reshape(count, block, rows)

    def one_block(pieces):
        query_block, mask_block = pieces
        scores = (
            jnp.einsum("hqd,hkd->hqk", query_block, heads_k, preferred_element_type=jnp.float32)
            * scale_factor
        )
        scores = jnp.where(mask_block[None], scores, -1e30)
        totals = jax.nn.logsumexp(scores, axis=-1, keepdims=True)
        probs = jnp.exp(scores - totals).astype(jnp.bfloat16)
        mixed = jnp.einsum("hqk,hkd->hqd", probs, heads_v, preferred_element_type=jnp.float32)
        return (mixed, totals)

    mixed, totals = lax.map(one_block, (query_blocks, mask_blocks))
    return (join_blocks(mixed).astype(jnp.bfloat16), totals)


def attention_backward(query, keys, values, allowed, totals, attended_grad):
    rows = query.shape[0]
    block = min(512, rows)
    count = rows // block
    scale_factor = HD ** (-0.5)
    heads_k = head_major(keys)
    heads_v = head_major(values)
    query_blocks = split_blocks(head_major(query), count, block)
    grad_blocks = split_blocks(head_major(attended_grad), count, block)
    mask_blocks = allowed.reshape(count, block, rows)

    def one_block(carry, pieces):
        key_acc, value_acc = carry
        query_block, grad_block, mask_block, total_block = pieces
        scores = (
            jnp.einsum("hqd,hkd->hqk", query_block, heads_k, preferred_element_type=jnp.float32)
            * scale_factor
        )
        scores = jnp.where(mask_block[None], scores, -1e30)
        probs = jnp.exp(scores - total_block)
        prob_low = probs.astype(jnp.bfloat16)
        prob_grad = jnp.einsum(
            "hqd,hkd->hqk", grad_block, heads_v, preferred_element_type=jnp.float32
        )
        weighted = jnp.sum(probs * prob_grad, axis=-1, keepdims=True)
        score_grad = (probs * (prob_grad - weighted)).astype(jnp.bfloat16)
        query_part = (
            jnp.einsum("hqk,hkd->hqd", score_grad, heads_k, preferred_element_type=jnp.float32)
            * scale_factor
        )
        key_acc = (
            key_acc
            + jnp.einsum(
                "hqk,hqd->hkd", score_grad, query_block, preferred_element_type=jnp.float32
            )
            * scale_factor
        )
        value_acc = value_acc + jnp.einsum(
            "hqk,hqd->hkd", prob_low, grad_block, preferred_element_type=jnp.float32
        )
        return ((key_acc, value_acc), query_part.astype(jnp.bfloat16))

    empty = jnp.zeros(heads_k.shape, jnp.float32)
    (key_acc, value_acc), query_parts = lax.scan(
        one_block, (empty, empty), (query_blocks, grad_blocks, mask_blocks, totals)
    )
    return (
        join_blocks(query_parts),
        row_major(key_acc).astype(jnp.bfloat16),
        row_major(value_acc).astype(jnp.bfloat16),
    )


def forward_pass(layer_input, segments, weights):
    (
        norm1_gain,
        norm1_bias,
        w_query,
        b_query,
        w_key,
        w_value,
        b_value,
        w_out,
        b_out,
        gate1_w,
        gate1_b,
        norm2_gain,
        norm2_bias,
        w_in,
        b_in,
        w_back,
        b_back,
        gate2_w,
        gate2_b,
    ) = weights
    start_col = lax.axis_index("tensor") * gate1_w.shape[0]
    inputs = layer_input.astype(jnp.float32)
    normed_part, unit_one, inverse_one = norm_forward(
        inputs, norm1_gain.astype(jnp.float32), norm1_bias.astype(jnp.float32)
    )
    normed_low = normed_part.astype(jnp.bfloat16)
    normed = lax.all_gather(normed_low, "tensor", axis=0, tiled=True)
    query = (matmul(normed, w_query) + b_query.astype(jnp.float32)).astype(jnp.bfloat16)
    keys = matmul(normed, w_key).astype(jnp.bfloat16)
    values = (matmul(normed, w_value) + b_value.astype(jnp.float32)).astype(jnp.bfloat16)
    allowed = build_mask(segments[0])
    attended, totals = attention_forward(query, keys, values, allowed)
    gate_rows = lax.dynamic_slice_in_dim(normed, start_col, gate1_w.shape[0], 1)
    branch_part, logit_one = (
        lax.psum_scatter(matmul(attended, w_out), "tensor", scatter_dimension=0, tiled=True),
        lax.psum_scatter(matmul(gate_rows, gate1_w), "tensor", scatter_dimension=0, tiled=True),
    )
    branch = branch_part + b_out.astype(jnp.float32)
    gate_one = jax.nn.sigmoid(logit_one + gate1_b.astype(jnp.float32))
    middle = inputs + gate_one * branch
    normed_two_part, unit_two, inverse_two = norm_forward(
        middle, norm2_gain.astype(jnp.float32), norm2_bias.astype(jnp.float32)
    )
    normed_two = lax.all_gather(normed_two_part.astype(jnp.bfloat16), "tensor", axis=0, tiled=True)
    hidden_input = matmul(normed_two, w_in) + b_in.astype(jnp.float32)
    hidden = smooth_unit(hidden_input).astype(jnp.bfloat16)
    gate_rows_two = lax.dynamic_slice_in_dim(normed_two, start_col, gate2_w.shape[0], 1)
    ffn_part, logit_two = (
        lax.psum_scatter(matmul(hidden, w_back), "tensor", scatter_dimension=0, tiled=True),
        lax.psum_scatter(matmul(gate_rows_two, gate2_w), "tensor", scatter_dimension=0, tiled=True),
    )
    ffn_out = ffn_part + b_back.astype(jnp.float32)
    gate_two = jax.nn.sigmoid(logit_two + gate2_b.astype(jnp.float32))
    result = middle + gate_two * ffn_out
    saved = (
        normed,
        normed_low,
        query,
        keys,
        values,
        allowed,
        attended,
        totals,
        branch,
        gate_one,
        unit_one,
        inverse_one,
        normed_two,
        hidden,
        hidden_input,
        ffn_out,
        gate_two,
        unit_two,
        inverse_two,
    )
    return (result, saved)


def body(
    layer_input,
    segments,
    norm1_gain,
    norm1_bias,
    w_query,
    b_query,
    w_key,
    w_value,
    b_value,
    w_out,
    b_out,
    gate1_w,
    gate1_b,
    norm2_gain,
    norm2_bias,
    w_in,
    b_in,
    w_back,
    b_back,
    gate2_w,
    gate2_b,
    cotangent,
):
    weights = (
        norm1_gain,
        norm1_bias,
        w_query,
        b_query,
        w_key,
        w_value,
        b_value,
        w_out,
        b_out,
        gate1_w,
        gate1_b,
        norm2_gain,
        norm2_bias,
        w_in,
        b_in,
        w_back,
        b_back,
        gate2_w,
        gate2_b,
    )
    result, saved = forward_pass(layer_input, segments, weights)
    barrier = lax.optimization_barrier((layer_input, weights))
    unused, saved = forward_pass(barrier[0], segments, barrier[1])
    (
        normed,
        normed_low,
        query,
        keys,
        values,
        allowed,
        attended,
        totals,
        branch,
        gate_one,
        unit_one,
        inverse_one,
        normed_two,
        hidden,
        hidden_input,
        ffn_out,
        gate_two,
        unit_two,
        inverse_two,
    ) = saved
    start_col = lax.axis_index("tensor") * gate1_w.shape[0]
    upstream = cotangent.astype(jnp.float32)
    ffn_grad = (gate_two * upstream).astype(jnp.bfloat16)
    logit_two_grad = (upstream * ffn_out * (gate_two * (1.0 - gate_two))).astype(jnp.bfloat16)
    ffn_grad_all, logit_two_all = (
        lax.all_gather(ffn_grad, "tensor", axis=0, tiled=True),
        lax.all_gather(logit_two_grad, "tensor", axis=0, tiled=True),
    )
    grad_b_back = column_sum(ffn_grad_all)
    grad_gate2_b = column_sum(logit_two_all)
    grad_w_back = inner_left(hidden, ffn_grad_all)
    unused_value, smooth_pull = jax.vjp(smooth_unit, hidden_input)
    hidden_grad = smooth_pull(outer_right(ffn_grad_all, w_back))[0].astype(jnp.bfloat16)
    grad_w_in = inner_left(normed_two, hidden_grad)
    grad_b_in = column_sum(hidden_grad)
    rows_two = lax.dynamic_slice_in_dim(normed_two, start_col, gate2_w.shape[0], 1)
    grad_gate2_w = inner_left(rows_two, logit_two_all)
    normed_two_grad = place_columns(
        outer_right(hidden_grad, w_in), outer_right(logit_two_all, gate2_w), start_col
    )
    normed_two_share = lax.psum_scatter(normed_two_grad, "tensor", scatter_dimension=0, tiled=True)
    middle_back, grad_norm2_gain, grad_norm2_bias = norm_backward(
        normed_two_share, unit_two, inverse_two, norm2_gain.astype(jnp.float32)
    )
    middle_grad = upstream + middle_back
    ffn_grads = (grad_w_in, grad_b_in, grad_w_back, grad_b_back, grad_gate2_w, grad_gate2_b)
    branch_grad = (gate_one * middle_grad).astype(jnp.bfloat16)
    logit_one_grad = (middle_grad * branch * (gate_one * (1.0 - gate_one))).astype(jnp.bfloat16)
    grad_b_out = column_sum(branch_grad)
    grad_gate1_b = column_sum(logit_one_grad)
    branch_all, logit_one_all = (
        lax.all_gather(branch_grad, "tensor", axis=0, tiled=True),
        lax.all_gather(logit_one_grad, "tensor", axis=0, tiled=True),
    )
    grad_w_out = inner_left(attended, branch_all)
    attended_grad = outer_right(branch_all, w_out).astype(jnp.bfloat16)
    rows_one = lax.dynamic_slice_in_dim(normed, start_col, gate1_w.shape[0], 1)
    grad_gate1_w = inner_left(rows_one, logit_one_all)
    query_grad, keys_grad, values_grad = attention_backward(
        query, keys, values, allowed, totals, attended_grad
    )
    grad_w_query = inner_left(normed, query_grad)
    grad_b_query = column_sum(query_grad)
    grad_w_key = inner_left(normed, keys_grad)
    grad_w_value = inner_left(normed, values_grad)
    grad_b_value = column_sum(values_grad)
    normed_grad = (
        outer_right(query_grad, w_query)
        + outer_right(keys_grad, w_key)
        + outer_right(values_grad, w_value)
    )
    normed_grad = place_columns(normed_grad, outer_right(logit_one_all, gate1_w), start_col)
    normed_share = lax.psum_scatter(
        normed_grad.astype(jnp.bfloat16), "tensor", scatter_dimension=0, tiled=True
    ).astype(jnp.float32)
    input_back, grad_norm1_gain, grad_norm1_bias = norm_backward(
        normed_share, unit_one, inverse_one, norm1_gain.astype(jnp.float32)
    )
    input_grad = middle_grad + input_back
    norm_sums = lax.psum(
        (
            grad_norm1_gain,
            grad_norm1_bias,
            grad_norm2_gain,
            grad_norm2_bias,
            grad_b_out,
            grad_gate1_b,
        ),
        ("dp", "tensor"),
    )
    attention_grads = (
        grad_w_query,
        grad_b_query,
        grad_w_key,
        grad_w_value,
        grad_b_value,
        grad_w_out,
        grad_gate1_w,
    )
    every_grad = lax.psum(
        (
            grad_w_query,
            grad_b_query,
            grad_w_key,
            grad_w_value,
            grad_b_value,
            grad_w_out,
            grad_gate1_w,
            grad_w_in,
            grad_b_in,
            grad_w_back,
            grad_b_back,
            grad_gate2_w,
            grad_gate2_b,
        ),
        "dp",
    )
    attention_grads = every_grad[0:7]
    ffn_grads = every_grad[7:13]
    return (
        result.astype(jnp.bfloat16),
        input_grad,
        norm_sums[0],
        norm_sums[1],
        attention_grads[0],
        attention_grads[1],
        attention_grads[2],
        attention_grads[3],
        attention_grads[4],
        attention_grads[5],
        norm_sums[4],
        attention_grads[6],
        norm_sums[5],
        norm_sums[2],
        norm_sums[3],
        ffn_grads[0],
        ffn_grads[1],
        ffn_grads[2],
        ffn_grads[3],
        ffn_grads[4],
        ffn_grads[5],
    )


def solution(mesh):
    placed = (
        P(("dp", "tensor"), None),
        P("dp", None),
        P(),
        P(),
        P(None, "tensor"),
        P("tensor"),
        P(None, "tensor"),
        P(None, "tensor"),
        P("tensor"),
        P("tensor", None),
        P(),
        P("tensor", None),
        P(),
        P(),
        P(),
        P(None, "tensor"),
        P("tensor"),
        P("tensor", None),
        P(),
        P("tensor", None),
        P(),
        P(("dp", "tensor"), None),
    )
    return jax.shard_map(
        body,
        mesh=mesh,
        in_specs=placed,
        out_specs=(
            P(("dp", "tensor"), None),
            P(("dp", "tensor"), None),
            P(),
            P(),
            P(None, "tensor"),
            P("tensor"),
            P(None, "tensor"),
            P(None, "tensor"),
            P("tensor"),
            P("tensor", None),
            P(),
            P("tensor", None),
            P(),
            P(),
            P(),
            P(None, "tensor"),
            P("tensor"),
            P("tensor", None),
            P(),
            P("tensor", None),
            P(),
        ),
        check_vma=False,
    )
```

profile of v0, /device:TPU:0, one launch (start us, length us, event | category | flops | bytes accessed | tf_op | source)
XLA Modules:
  0.0 718.7 jit_solution(1008536278620861501)
XLA Ops:
  16.1 1.9 fusion.52
  18.0 14.4 %all-gather.13.cloned.1.call-done = bf16[1024,512]{1,0:T(8,128)(2,1)} async-done(((bf16[256,512]{1,0:T(8,128)(2,1)}), bf16[1024,512]{1,0:T(8,128)(2,1)}) %all-gather.13.cloned.1.call-update) | async-done | bytes 1048592 | tf_op jit(solution)/shard_map/all_gather | solution.py:186
  36.2 8.7 %while.38 = (s32[]{:T(128)}, bf16[2,2,512,64]{2,3,1,0:T(8,128)(2,1)}, f32[2,2,512,1]{2,1,3,0:T(2,128)S(1)}, pred[2,512,1024]{2,1,0:T(8,128)(4,1)S(1)}, bf16[2,2,...) while((s32[]{:T(128)}, ...), condition=%wide.region_18.19_spmd, body=%wide.region_15.18_spmd.sunk | while | flops 279977984 | bytes 18268324 | solution.py:101
  48.9 2.7 fusion.116
  54.8 25.5 %reduce-scatter.21.cloned.1.call-done = f32[256,512]{1,0:T(8,128)} async-done(((f32[1024,512]{1,0:T(8,128)}), f32[256,512]{1,0:T(8,128)}) %reduce-scatter.21.cloned.1.call-update) | async-done | bytes 524304 | tf_op jit(solution)/shard_map/reduce_scatter | solution.py:194
  80.3 34.1 %reduce-scatter.19.cloned.1.call-done = f32[256,512]{1,0:T(8,128)} async-done(((f32[1024,512]{1,0:T(8,128)}), f32[256,512]{1,0:T(8,128)}) %reduce-scatter.19.cloned.1.call-update) | async-done | bytes 524304 | tf_op jit(solution)/shard_map/reduce_scatter | solution.py:195
  118.3 16.8 %all-gather.15.cloned.1.call-done = bf16[1024,512]{1,0:T(8,128)(2,1)} async-done(((bf16[256,512]{1,0:T(8,128)(2,1)}), bf16[1024,512]{1,0:T(8,128)(2,1)}) %all-gather.15.cloned.1.call-update) | async-done | bytes 1048592 | tf_op jit(solution)/shard_map/all_gather | solution.py:203
  135.1 2.7 fusion.112
  138.6 30.8 %reduce-scatter.23.cloned.1.call-done = f32[256,512]{1,0:T(8,128)} async-done(((f32[1024,512]{1,0:T(8,128)}), f32[256,512]{1,0:T(8,128)}) %reduce-scatter.23.cloned.1.call-update) | async-done | bytes 524304 | tf_op jit(solution)/shard_map/reduce_scatter | solution.py:209
  169.5 2.0 fusion.100
  172.8 3.4 fusion.134
  176.2 12.2 %all-gather.17.cloned.1.call-done = bf16[1024,512]{1,0:T(8,128)(2,1)} async-done(((bf16[256,512]{1,0:T(8,128)(2,1)}), bf16[1024,512]{1,0:T(8,128)(2,1)}) %all-gather.17.cloned.1.call-update) | async-done | bytes 1048592 | tf_op jit(solution)/shard_map/all_gather | solution.py:312
  188.4 5.5 convert_reduce_fusion.2
  194.8 2.0 fusion.136
  198.2 30.3 %reduce-scatter.25.cloned.1.call-done = f32[256,512]{1,0:T(8,128)} async-done(((f32[1024,512]{1,0:T(8,128)}), f32[256,512]{1,0:T(8,128)}) %reduce-scatter.25.cloned.1.call-update) | async-done | bytes 524304 | tf_op jit(solution)/shard_map/reduce_scatter | solution.py:208
  228.5 2.2 fusion.102
  230.9 3.4 fusion.135
  234.4 13.2 %all-gather.19.cloned.1.call-done = bf16[1024,512]{1,0:T(8,128)(2,1)} async-done(((bf16[256,512]{1,0:T(8,128)(2,1)}), bf16[1024,512]{1,0:T(8,128)(2,1)}) %all-gather.19.cloned.1.call-update) | async-done | bytes 1048592 | tf_op jit(solution)/shard_map/all_gather | solution.py:313
  247.6 2.7 fusion.69
  251.1 30.8 %reduce-scatter.27.cloned.1.call-done = f32[256,512]{1,0:T(8,128)} async-done(((f32[1024,512]{1,0:T(8,128)}), f32[256,512]{1,0:T(8,128)}) %reduce-scatter.27.cloned.1.call-update) | async-done | bytes 524304 | tf_op jit(solution)/shard_map/reduce_scatter | solution.py:327
  281.9 2.1 multiply_reduce_fusion.1
  284.1 3.3 convert_reduce_fusion.6
  289.6 16.1 %all-gather.21.cloned.1.call-done = bf16[1024,512]{1,0:T(8,128)(2,1)} async-done(((bf16[256,512]{1,0:T(8,128)(2,1)}), bf16[1024,512]{1,0:T(8,128)(2,1)}) %all-gather.21.cloned.1.call-update) | async-done | bytes 1048592 | tf_op jit(solution)/shard_map/all_gather | solution.py:338
  305.7 2.4 convolution_convert_fusion
  311.7 16.5 %while.39 = (s32[]{:T(128)}, f32[2,1024,64]{1,2,0:T(8,128)}, f32[2,1024,64]{1,2,0:T(8,128)}, bf16[2,2,512,64]{2,3,1,0:T(8,128)(2,1)}, pred[2,512,1024]{2,1,0:T(8...) while((s32[]{:T(128)}, f32[2,1024,64]{1,2,0:T(8,128)}, ...), condition=%wide.region_29.30_spmd.clone, body=%wide.region_27.29_spmd.clone.sunk | while | flops 687602688 | bytes 50229632 | solution.py:148
  334.2 2.7 fusion.68
  336.9 2.7 convert_element_type.273
  343.1 21.6 %reduce-scatter.29.cloned.1.call-done = bf16[256,512]{1,0:T(8,128)(2,1)} async-done(((bf16[1024,512]{1,0:T(8,128)(2,1)}), bf16[256,512]{1,0:T(8,128)(2,1)}) %reduce-scatter.29.cloned.1.call-update) | async-done | bytes 262160 | tf_op jit(solution)/shard_map/reduce_scatter | solution.py:359
  364.7 1.9 fusion.105
  366.6 2.4 fusion.93
  370.4 15.5 %all-gather.9.cloned.1.call-done = bf16[1024,512]{1,0:T(8,128)(2,1)} async-done(((bf16[256,512]{1,0:T(8,128)(2,1)}), bf16[1024,512]{1,0:T(8,128)(2,1)}) %all-gather.9.cloned.1.call-update) | async-done | bytes 1048592 | tf_op jit(solution)/shard_map/all_gather | solution.py:186
  385.9 2.4 fusion.71
  391.9 2.7 fusion.108
  394.9 2.4 convolution_convert_fusion.2
  397.3 2.4 fusion.72
  400.4 10.8 %while.37 = (s32[]{:T(128)}, bf16[2,2,512,64]{2,3,1,0:T(8,128)(2,1)}, pred[2,512,1024]{2,1,0:T(8,128)(4,1)S(1)}, bf16[2,2,512,64]{2,3,1,0:T(8,128)(2,1)}, bf16[2...) while((s32[]{:T(128)}, bf16[2,2,512,64]{2,3,1,0:T(8,128)(2,1)}, ...), condition=%wide.region_6.7_spmd, body=%wide.region_3.0_spmd.sunk | while | flops 279973888 | bytes 19304628 | solution.py:101
  400.5 2.1 fusion.236
  405.9 2.1 fusion.236
  414.5 11.7 %reduce-scatter.11.cloned.1.call-done = f32[256,512]{1,0:T(8,128)} async-done(((f32[1024,512]{1,0:T(8,128)}), f32[256,512]{1,0:T(8,128)}) %reduce-scatter.11.cloned.1.call-update) | async-done | bytes 524304 | tf_op jit(solution)/shard_map/reduce_scatter | solution.py:195
  426.2 34.0 %reduce-scatter.13.cloned.1.call-done = f32[256,512]{1,0:T(8,128)} async-done(((f32[1024,512]{1,0:T(8,128)}), f32[256,512]{1,0:T(8,128)}) %reduce-scatter.13.cloned.1.call-update) | async-done | bytes 524304 | tf_op jit(solution)/shard_map/reduce_scatter | solution.py:194
  462.9 16.8 %all-gather.11.cloned.1.call-done = bf16[1024,512]{1,0:T(8,128)(2,1)} async-done(((bf16[256,512]{1,0:T(8,128)(2,1)}), bf16[1024,512]{1,0:T(8,128)(2,1)}) %all-gather.11.cloned.1.call-update) | async-done | bytes 1048592 | tf_op jit(solution)/shard_map/all_gather | solution.py:203
  479.7 4.1 fusion.70
  484.7 2.7 fusion.106
  487.4 3.4 fusion.144
  501.2 22.1 %all-reduce.1 = (f32[128]{0:T(128)}, f32[128]{0:T(128)}, f32[512]{0:T(512)}, f32[512]{0:T(512)}, f32[512]{0:T(512)}) all-reduce(f32[128]{0:T(128)S(1)} %reduce_sum.253, f32[128]{0:T(128)S(1)} %reduce_sum.255, f32[512]{0:T(512)S(1)} %copy-done.71, f32[512]{0:T(512)S(1)} %convert_reduce_fusion.1, ...), channel_id=1, replica_groups=mesh['dp'=8,'tensor'=4] {'dp'}, use_global_device_ids=true, to_apply=%region_39.40 | all-reduce | flops 1792 | bytes 14336 | tf_op jit(solution)/shard_map/psum | solution.py:386
  523.4 37.1 %all-reduce = (f32[512]{0:T(512)}, f32[512]{0:T(512)}, f32[512]{0:T(512)}, f32[512]{0:T(512)}, f32[512]{0:T(512)}, /*index=5*/f32[512]{0:T(512)}) all-reduce(f32[512]{0:T(512)S(1)} %copy-done.62, f32[512]{0:T(512)S(1)} %copy-done.63, f32[512]{0:T(512)S(1)} %copy-done.61, ...), channel_id=1, replica_groups=mesh['dp'=8,'tensor'=4] {'dp','tensor'}, use_global_device_ids=true, to_apply=%region_34.35 | all-reduce | flops 3072 | bytes 24576 | tf_op jit(solution)/shard_map/psum | solution.py:366
  560.4 2.2 add_convert_fusion.1
  562.6 139.3 %all-reduce.5.cloned.1.call-done = (f32[512,128]{1,0:T(8,128)}, f32[512,128]{1,0:T(8,128)}, f32[512,128]{1,0:T(8,128)}, f32[128,512]{1,0:T(8,128)}, f32[128,512]...) async-done(((f32[512,128]{1,0:T(8,128)}, f32[512,128]{1,0:T(8,128)}, f32[512,128]{1,0:T(8,128)}, f32[128,512]{1,0:T(8,128)}, ...) | async-done | bytes 3670032 | tf_op jit(solution)/shard_map/psum | solution.py:386
  (350 shorter events, 108.4 us)
Async XLA Ops:
  7.2 181.2 %copy-start = (bf16[512,512]{1,0:T(8,128)(2,1)S(1)}, bf16[512,512]{1,0:T(8,128)(2,1)}, u32[]{:S(2)}) copy-start(bf16[512,512]{1,0:T(8,128)(2,1)} %param.45) | copy-start | bytes 1572868
  7.2 25.2 %copy-start.23 = (bf16[512,128]{1,0:T(8,128)(2,1)S(1)}, bf16[512,128]{1,0:T(8,128)(2,1)}, u32[]{:S(2)}) copy-start(bf16[512,128]{1,0:T(8,128)(2,1)} %param.32) | copy-start | bytes 393220
  7.2 25.2 %all-gather.13.cloned.1.call-start = ((), (), s32[]{:S(2)}) async-start(), calls=%async_computation.16 | async-start | bytes 1310720 | tf_op jit(solution)/shard_map/all_gather | solution.py:186
  8.4 25.8 %copy-start.48 = (f32[256]{0:T(256)}, f32[256]{0:T(256)S(1)}, u32[]{:S(2)}) copy-start(f32[256]{0:T(256)S(1)} %broadcast_multiply_fusion.5) | copy-start | bytes 3076
  9.6 24.7 %copy-start.52 = (f32[256]{0:T(256)}, f32[256]{0:T(256)S(1)}, u32[]{:S(2)}) copy-start(f32[256]{0:T(256)S(1)} %add_rsqrt_fusion.1) | copy-start | bytes 3076
  11.0 23.5 %copy-start.25 = (bf16[512,128]{1,0:T(8,128)(2,1)S(1)}, bf16[512,128]{1,0:T(8,128)(2,1)}, u32[]{:S(2)}) copy-start(bf16[512,128]{1,0:T(8,128)(2,1)} %param.34) | copy-start | bytes 393220
  12.9 67.5 %reduce-scatter.21.cloned.1.call-start = ((), (), s32[]{:S(2)}) async-start(), calls=%async_computation.18 | async-start | bytes 2621440 | tf_op jit(solution)/shard_map/reduce_scatter | solution.py:194
  18.0 17.0 %copy-start.27 = (bf16[512,128]{1,0:T(8,128)(2,1)S(1)}, bf16[512,128]{1,0:T(8,128)(2,1)}, u32[]{:S(2)}) copy-start(bf16[512,128]{1,0:T(8,128)(2,1)} %param.35) | copy-start | bytes 393220
  36.2 10.7 %copy-start.22 = (bf16[128,512]{1,0:T(8,128)(2,1)S(1)}, bf16[128,512]{1,0:T(8,128)(2,1)}, u32[]{:S(2)}) copy-start(bf16[128,512]{1,0:T(8,128)(2,1)} %param.37) | copy-start | bytes 393220
  44.9 3.9 copy-start.6
  48.8 65.7 %reduce-scatter.19.cloned.1.call-start = ((), (), s32[]{:S(2)}) async-start(), calls=%async_computation.17 | async-start | bytes 2621440 | tf_op jit(solution)/shard_map/reduce_scatter | solution.py:195
  48.8 65.6 %copy-start.2 = (bf16[256,512]{1,0:T(8,128)(2,1)S(1)}, bf16[256,512]{1,0:T(8,128)(2,1)}, u32[]{:S(2)}) copy-start(bf16[256,512]{1,0:T(8,128)(2,1)} %param.28) | copy-start | bytes 786436
  51.6 83.6 %all-gather.15.cloned.1.call-start = ((), (), s32[]{:S(2)}) async-start(), calls=%async_computation.19 | async-start | bytes 1310720 | tf_op jit(solution)/shard_map/all_gather | solution.py:203
  52.3 63.7 %copy-start.51 = (f32[512]{0:T(512)}, f32[512]{0:T(512)S(1)}, u32[]{:S(2)}) copy-start(f32[512]{0:T(512)S(1)} %convert_element_type.253) | copy-start | bytes 6148
  116.0 21.9 %copy-start.50 = (f32[256]{0:T(256)}, f32[256]{0:T(256)S(1)}, u32[]{:S(2)}) copy-start(f32[256]{0:T(256)S(1)} %broadcast_multiply_fusion.4) | copy-start | bytes 3076
  118.2 51.2 %reduce-scatter.23.cloned.1.call-start = ((), (), s32[]{:S(2)}) async-start(), calls=%async_computation.20 | async-start | bytes 2621440 | tf_op jit(solution)/shard_map/reduce_scatter | solution.py:209
  137.9 50.5 %all-gather.17.cloned.1.call-start = ((), (), s32[]{:S(2)}) async-start(), calls=%async_computation.21 | async-start | bytes 1310720 | tf_op jit(solution)/shard_map/all_gather | solution.py:312
  171.5 57.0 %reduce-scatter.25.cloned.1.call-start = ((), (), s32[]{:S(2)}) async-start(), calls=%async_computation.22 | async-start | bytes 2621440 | tf_op jit(solution)/shard_map/reduce_scatter | solution.py:208
  196.9 50.7 %all-gather.19.cloned.1.call-start = ((), (), s32[]{:S(2)}) async-start(), calls=%async_computation.23 | async-start | bytes 1310720 | tf_op jit(solution)/shard_map/all_gather | solution.py:313
  230.7 51.2 %reduce-scatter.27.cloned.1.call-start = ((), (), s32[]{:S(2)}) async-start(), calls=%async_computation.24 | async-start | bytes 2621440 | tf_op jit(solution)/shard_map/reduce_scatter | solution.py:327
  250.3 55.4 %all-gather.21.cloned.1.call-start = ((), (), s32[]{:S(2)}) async-start(), calls=%async_computation.25 | async-start | bytes 1310720 | tf_op jit(solution)/shard_map/all_gather | solution.py:338
  281.9 5.5 copy-start.11
  288.8 45.3 %all-gather.23.cloned.1.call-start = ((), (), s32[]{:S(2)}) async-start(), calls=%async_computation.26 | async-start | bytes 1310720 | tf_op jit(solution)/shard_map/all_gather | solution.py:339
  289.6 75.1 %reduce-scatter.29.cloned.1.call-start = ((), (), s32[]{:S(2)}) async-start(), calls=%async_computation.27 | async-start | bytes 1310720 | tf_op jit(solution)/shard_map/reduce_scatter | solution.py:359
  336.9 27.8 %copy-start.49 = (f32[256]{0:T(256)S(1)}, f32[256]{0:T(256)}, u32[]{:S(2)}) copy-start(f32[256]{0:T(256)} %copy-done.48) | copy-start | bytes 3076
  336.9 27.8 %copy-start.53 = (f32[256]{0:T(256)S(1)}, f32[256]{0:T(256)}, u32[]{:S(2)}) copy-start(f32[256]{0:T(256)} %copy-done.52) | copy-start | bytes 3076
  339.6 46.3 %all-gather.9.cloned.1.call-start = ((), (), s32[]{:S(2)}) async-start(), calls=%async_computation.10 | async-start | bytes 1310720 | tf_op jit(solution)/shard_map/all_gather | solution.py:186
  369.0 57.2 %reduce-scatter.11.cloned.1.call-start = ((), (), s32[]{:S(2)}) async-start(), calls=%async_computation.11 | async-start | bytes 2621440 | tf_op jit(solution)/shard_map/reduce_scatter | solution.py:195
  394.6 65.6 %reduce-scatter.13.cloned.1.call-start = ((), (), s32[]{:S(2)}) async-start(), calls=%async_computation.12 | async-start | bytes 2621440 | tf_op jit(solution)/shard_map/reduce_scatter | solution.py:194
  414.4 48.5 %copy-start.68 = (bf16[512]{0:T(512)(128)(2,1)S(1)}, bf16[512]{0:T(512)(128)(2,1)}, u32[]{:S(2)}) copy-start(bf16[512]{0:T(512)(128)(2,1)} %param.44) | copy-start | bytes 3076
  414.4 65.3 %copy-start.21 = (bf16[512,512]{1,0:T(8,128)(2,1)S(1)}, bf16[512,512]{1,0:T(8,128)(2,1)}, u32[]{:S(2)}) copy-start(bf16[512,512]{1,0:T(8,128)(2,1)} %param.43) | copy-start | bytes 1572868
  414.4 65.3 %all-gather.11.cloned.1.call-start = ((), (), s32[]{:S(2)}) async-start(), calls=%async_computation.13 | async-start | bytes 1310720 | tf_op jit(solution)/shard_map/all_gather | solution.py:203
  461.7 22.1 %copy-start.9 = (f32[256,512]{1,0:T(8,128)}, f32[256,512]{1,0:T(8,128)S(1)}, u32[]{:S(2)}) copy-start(f32[256,512]{1,0:T(8,128)S(1)} %get-tuple-element.332) | copy-start | bytes 1572868
  462.8 97.6 %reduce-scatter.17.cloned.1.call-start = ((), (), s32[]{:S(2)}) async-start(), calls=%async_computation.15 | async-start | bytes 2621440 | tf_op jit(solution)/shard_map/reduce_scatter | solution.py:208
  483.8 76.7 %reduce-scatter.15.cloned.1.call-start = ((), (), s32[]{:S(2)}) async-start(), calls=%async_computation.14 | async-start | bytes 2621440 | tf_op jit(solution)/shard_map/reduce_scatter | solution.py:209
  487.4 214.6 %all-reduce.5.cloned.1.call-start = ((), (), s32[]{:S(2)}) async-start(), calls=%async_computation.28 | async-start | bytes 7340032 | tf_op jit(solution)/shard_map/psum | solution.py:386
  487.4 3.4 copy-start.16
  487.4 3.4 copy-start.30
  499.9 23.4 %copy-start.58 = (f32[512]{0:T(512)S(1)}, f32[512]{0:T(512)}, u32[]{:S(2)}) copy-start(f32[512]{0:T(512)} %get-tuple-element.247) | copy-start | bytes 6148
  499.9 23.4 %copy-start.59 = (f32[512]{0:T(512)S(1)}, f32[512]{0:T(512)}, u32[]{:S(2)}) copy-start(f32[512]{0:T(512)} %get-tuple-element.252) | copy-start | bytes 6148
  499.9 23.4 %copy-start.60 = (f32[512]{0:T(512)S(1)}, f32[512]{0:T(512)}, u32[]{:S(2)}) copy-start(f32[512]{0:T(512)} %get-tuple-element.324) | copy-start | bytes 6148
  499.9 23.4 %copy-start.61 = (f32[512]{0:T(512)S(1)}, f32[512]{0:T(512)}, u32[]{:S(2)}) copy-start(f32[512]{0:T(512)} %get-tuple-element.327) | copy-start | bytes 6148
  499.9 23.4 %copy-start.62 = (f32[512]{0:T(512)S(1)}, f32[512]{0:T(512)}, u32[]{:S(2)}) copy-start(f32[512]{0:T(512)} %get-tuple-element.250) | copy-start | bytes 6148
  499.9 23.4 %copy-start.63 = (f32[512]{0:T(512)S(1)}, f32[512]{0:T(512)}, u32[]{:S(2)}) copy-start(f32[512]{0:T(512)} %get-tuple-element.254) | copy-start | bytes 6148
  499.9 60.5 %copy-start.10 = (f32[256,512]{1,0:T(8,128)S(1)}, f32[256,512]{1,0:T(8,128)}, u32[]{:S(2)}) copy-start(f32[256,512]{1,0:T(8,128)} %copy-done.9) | copy-start | bytes 1572868
  701.9 6.9 copy-start.46
  701.9 7.6 %copy-start.34 = (f32[512,512]{1,0:T(8,128)S(1)}, f32[512,512]{1,0:T(8,128)}, u32[]{:S(2)}) copy-start(f32[512,512]{1,0:T(8,128)} %get-tuple-element.593) | copy-start | bytes 3145732
  703.7 6.8 copy-start.33
  (57 other events, 81.4 us)
Sparse Core Ops, SparseCore 0:
  13.0 19.4 all-gather.12
  48.9 31.4 reduce-scatter.20
  83.0 31.3 reduce-scatter.18
  118.4 16.7 all-gather.14
  138.0 31.4 reduce-scatter.22
  171.6 16.7 all-gather.16
  197.0 31.4 reduce-scatter.24
  230.8 16.7 all-gather.18
  250.5 31.4 reduce-scatter.26
  289.0 16.7 all-gather.20
  307.9 16.7 all-gather.22
  339.7 24.8 reduce-scatter.28
  369.1 16.7 all-gather.8
  394.7 31.4 reduce-scatter.10
  428.7 31.4 reduce-scatter.12
  462.9 16.7 all-gather.10
  483.9 31.4 reduce-scatter.16
  517.9 31.5 reduce-scatter.14
  555.9 145.9 all-reduce.4
where the time goes:
time: 720 us; the launch traced here: 719 us
  waiting for transfers between devices  464 us (64%)
  matrix products  87.1 us (12%)
  blocking collectives  59.2 us (8%)
  other arithmetic  56.5 us (8%)
  local copies, waits for them, and re-layouts  35.3 us (5%)
  between operations  14.7 us (2%)
    psum x1, waiting for transfers between devices, body(): lax.psum((grad_w_query, grad_b_query, grad_w_key, grad_w_value, grad_b_va...  139 us
    reduce_scatter x2, waiting for transfers between devices, forward_pass(): lax.psum_scatter(matmul(attended, w_out), 'tensor', scatter_dimension=0,...  59.5 us
    reduce_scatter x2, waiting for transfers between devices, forward_pass(): lax.psum_scatter(matmul(gate_rows, gate1_w), 'tensor', scatter_dimension=...  45.8 us
    psum x1, blocking collectives, body(): lax.psum((grad_norm1_gain, grad_norm1_bias, grad_norm2_gain, grad_norm2_b...  37.1 us
    dot_general x15, matrix products, matmul(): return jnp.dot(left, right, preferred_element_type=jnp.float32)  33.9 us
    all_gather x2, waiting for transfers between devices, forward_pass(): lax.all_gather(normed_two_part.astype(jnp.bfloat16), 'tensor', axis=0, ti...  33.6 us
    reduce_scatter x1, waiting for transfers between devices, body(): lax.psum_scatter(normed_two_grad, 'tensor', scatter_dimension=0, tiled=True)  30.8 us
    reduce_scatter x2, waiting for transfers between devices, forward_pass(): lax.psum_scatter(matmul(gate_rows_two, gate2_w), 'tensor', scatter_dimens...  30.8 us
  transfers between devices with their start and end apart: 19, of which 16 were waited for; matrix products, arithmetic and copies ran while one was open for 12% of the time, Pallas kernels for 0%

commit v1 on v0

--- a/solution.py
+++ b/solution.py
@@ -156,6 +156,34 @@
 
 
 def forward_pass(layer_input, segments, weights):
+
+    def return_all_ports_now(axis_no, mine_x):
+        axis_tag = "tensor"
+        d_next = lax.axis_index(axis_tag)
+        opened = lax.axis_size(axis_tag)
+        local_now, f_now, reply = (opened, d_next, mine_x.shape[axis_no])
+        known = map(lambda s: (s, (s + 1) % local_now), range(local_now))
+        slots = list(known)
+        left_arr = map(lambda s: (s, (s - 1) % local_now), range(local_now))
+        row_out = jnp.zeros(
+            (*mine_x.shape[:axis_no], local_now * reply, *mine_x.shape[axis_no + 1 :]), mine_x.dtype
+        )
+        row_out = lax.dynamic_update_slice_in_dim(row_out, mine_x, f_now * reply, axis=axis_no)
+        local_out = lower = mine_x
+        z2 = local_now // 2
+        lanes = list(left_arr)
+        for hop_no in [*range(1, z2 + 1)]:
+            local_out = lax.ppermute(local_out, axis_name=axis_tag, perm=slots)
+            row_out = lax.dynamic_update_slice_in_dim(
+                row_out, local_out, (f_now - hop_no) % local_now * reply, axis=axis_no
+            )
+            if hop_no < local_now - z2:
+                lower = lax.ppermute(lower, axis_name=axis_tag, perm=lanes)
+                row_out = lax.dynamic_update_slice_in_dim(
+                    row_out, lower, (f_now + hop_no) % local_now * reply, axis=axis_no
+                )
+        return row_out
+
     (
         norm1_gain,
         norm1_bias,
@@ -183,7 +211,7 @@
         inputs, norm1_gain.astype(jnp.float32), norm1_bias.astype(jnp.float32)
     )
     normed_low = normed_part.astype(jnp.bfloat16)
-    normed = lax.all_gather(normed_low, "tensor", axis=0, tiled=True)
+    normed = return_all_ports_now(0, normed_low)
     query = (matmul(normed, w_query) + b_query.astype(jnp.float32)).astype(jnp.bfloat16)
     keys = matmul(normed, w_key).astype(jnp.bfloat16)
     values = (matmul(normed, w_value) + b_value.astype(jnp.float32)).astype(jnp.bfloat16)

time: 720 us -> 687 us (0.954)
  waiting for transfers between devices: 464 us -> 413 us
  local copies, waits for them, and re-layouts: 35.3 us -> 42.8 us
    all_gather x2 -> x0, waiting for transfers between devices: 29.9 us -> none  [forward_pass(): normed = lax.all_gather(normed_low, 'tensor', axis=0, tiled=True)]
    reduce_scatter x1, waiting for transfers between devices: 21.6 us -> 0.01 us  [body(): lax.psum_scatter(normed_grad.astype(jnp.bfloat16), 'tensor', scatter_dime...]
    ppermute x0 -> x6, waiting for transfers between devices: none -> 15.4 us  [the longest x4 15.4 us: return_all_ports_now(): local_out = lax.ppermute(local_out, axis_name=axis_tag, perm=slots)]
    all_gather x1, waiting for transfers between devices: 13.2 us -> 0.01 us  [body(): lax.all_gather(logit_two_grad, 'tensor', axis=0, tiled=True)]
    all_gather x2, waiting for transfers between devices: 33.6 us -> 21.1 us  [forward_pass(): lax.all_gather(normed_two_part.astype(jnp.bfloat16), 'tensor', axis=0, ti...]
    reduce_scatter x2, waiting for transfers between devices: 45.8 us -> 34.8 us  [forward_pass(): lax.psum_scatter(matmul(gate_rows, gate1_w), 'tensor', scatter_dimension=...]
    psum x1, waiting for transfers between devices: 139 us -> 150 us  [body(): lax.psum((grad_w_query, grad_b_query, grad_w_key, grad_w_value, grad_b_va...]
    reduce_scatter x2, waiting for transfers between devices: 30.8 us -> 41.5 us  [forward_pass(): lax.psum_scatter(matmul(gate_rows_two, gate2_w), 'tensor', scatter_dimens...]
  transfers between devices with their start and end apart: 19 -> 23, of which waited for: 16 -> 17; matrix products, arithmetic and copies ran while one was open for 12% -> 18% of each run, Pallas kernels for 0% -> 0%
where the time goes in v1:
time: 687 us; the launch traced here: 685 us
  waiting for transfers between devices  413 us (60%)
  matrix products  86 us (13%)
  other arithmetic  60.6 us (9%)
  blocking collectives  59.6 us (9%)
  local copies, waits for them, and re-layouts  42.8 us (6%)
  between operations  14.8 us (2%)
  starting transfers between devices  8.21 us (1%)
    psum x1, waiting for transfers between devices, body(): lax.psum((grad_w_query, grad_b_query, grad_w_key, grad_w_value, grad_b_va...  150 us
    reduce_scatter x2, waiting for transfers between devices, forward_pass(): lax.psum_scatter(matmul(attended, w_out), 'tensor', scatter_dimension=0,...  63.6 us
    reduce_scatter x2, waiting for transfers between devices, forward_pass(): lax.psum_scatter(matmul(gate_rows_two, gate2_w), 'tensor', scatter_dimens...  41.5 us
    psum x1, blocking collectives, body(): lax.psum((grad_norm1_gain, grad_norm1_bias, grad_norm2_gain, grad_norm2_b...  37.4 us
    reduce_scatter x2, waiting for transfers between devices, forward_pass(): lax.psum_scatter(matmul(gate_rows, gate1_w), 'tensor', scatter_dimension=...  34.8 us
    dot_general x15, matrix products, matmul(): return jnp.dot(left, right, preferred_element_type=jnp.float32)  32.7 us
    reduce_scatter x1, waiting for transfers between devices, body(): lax.psum_scatter(normed_two_grad, 'tensor', scatter_dimension=0, tiled=True)  30.8 us
    reduce_scatter x2, waiting for transfers between devices, forward_pass(): lax.psum_scatter(matmul(hidden, w_back), 'tensor', scatter_dimension=0, t...  26.7 us
  transfers between devices with their start and end apart: 23, of which 17 were waited for; matrix products, arithmetic and copies ran while one was open for 18% of the time, Pallas kernels for 0%

profile of v1, /device:TPU:0, one launch (start us, length us, event | category | flops | bytes accessed | tf_op | source)
XLA Modules:
  0.0 685.3 jit_solution(7844050310625490319)
XLA Ops:
  13.4 2.0 collective-permute-start.4
  16.5 3.2 collective-permute-done.3
  19.7 2.7 collective-permute-start.5
  29.0 8.7 %while.38 = (s32[]{:T(128)}, bf16[2,2,512,64]{2,3,1,0:T(8,128)(2,1)}, f32[2,2,512,1]{2,1,3,0:T(2,128)S(1)}, pred[2,512,1024]{2,1,0:T(8,128)(4,1)S(1)}, bf16[2,2,...) while((s32[]{:T(128)}, ...), condition=%wide.region_18.19_spmd, body=%wide.region_15.18_spmd.sunk | while | flops 279977984 | bytes 18268324 | solution.py:101
  41.7 2.7 fusion.116
  47.6 29.4 %reduce-scatter.21.cloned.1.call-done = f32[256,512]{1,0:T(8,128)} async-done(((f32[1024,512]{1,0:T(8,128)}), f32[256,512]{1,0:T(8,128)}) %reduce-scatter.21.cloned.1.call-update) | async-done | bytes 524304 | tf_op jit(solution)/shard_map/reduce_scatter | solution.py:222
  77.1 34.1 %reduce-scatter.19.cloned.1.call-done = f32[256,512]{1,0:T(8,128)} async-done(((f32[1024,512]{1,0:T(8,128)}), f32[256,512]{1,0:T(8,128)}) %reduce-scatter.19.cloned.1.call-update) | async-done | bytes 524304 | tf_op jit(solution)/shard_map/reduce_scatter | solution.py:223
  115.0 16.8 %all-gather.9.cloned.1.call-done = bf16[1024,512]{1,0:T(8,128)(2,1)} async-done(((bf16[256,512]{1,0:T(8,128)(2,1)}), bf16[1024,512]{1,0:T(8,128)(2,1)}) %all-gather.9.cloned.1.call-update) | async-done | bytes 1048592 | tf_op jit(solution)/shard_map/all_gather | solution.py:231
  131.8 2.7 fusion.112
  135.3 30.8 %reduce-scatter.23.cloned.1.call-done = f32[256,512]{1,0:T(8,128)} async-done(((f32[1024,512]{1,0:T(8,128)}), f32[256,512]{1,0:T(8,128)}) %reduce-scatter.23.cloned.1.call-update) | async-done | bytes 524304 | tf_op jit(solution)/shard_map/reduce_scatter | solution.py:237
  166.2 2.0 fusion.100
  169.5 3.4 fusion.136
  172.9 12.2 %all-gather.11.cloned.1.call-done = bf16[1024,512]{1,0:T(8,128)(2,1)} async-done(((bf16[256,512]{1,0:T(8,128)(2,1)}), bf16[1024,512]{1,0:T(8,128)(2,1)}) %all-gather.11.cloned.1.call-update) | async-done | bytes 1048592 | tf_op jit(solution)/shard_map/all_gather | solution.py:340
  185.1 5.5 convert_reduce_fusion.2
  191.6 2.0 fusion.138
  198.6 26.7 %reduce-scatter.25.cloned.1.call-done = f32[256,512]{1,0:T(8,128)} async-done(((f32[1024,512]{1,0:T(8,128)}), f32[256,512]{1,0:T(8,128)}) %reduce-scatter.25.cloned.1.call-update) | async-done | bytes 524304 | tf_op jit(solution)/shard_map/reduce_scatter | solution.py:236
  225.3 2.2 fusion.102
  232.7 8.4 %collective-permute-done = bf16[256,512]{1,0:T(8,128)(2,1)} collective-permute-done((bf16[256,512]{1,0:T(8,128)(2,1)}, bf16[256,512]{1,0:T(8,128)(2,1)}, u32[]{:S(2)}, u32[]{:S(2)}) %collective-permute-start) | collective-permute-done | bytes 262176 | tf_op jit(solution)/shard_map/ppermute | solution.py:176
  246.2 2.0 collective-permute-done.2
  249.9 2.4 fusion.71
  252.3 1.9 reshape.261
  255.9 2.8 fusion.108
  258.7 2.4 convolution_convert_fusion.2
  261.1 2.5 fusion.72
  264.3 10.8 %while.37 = (s32[]{:T(128)}, bf16[2,2,512,64]{2,3,1,0:T(8,128)(2,1)}, pred[2,512,1024]{2,1,0:T(8,128)(4,1)S(1)}, bf16[2,2,512,64]{2,3,1,0:T(8,128)(2,1)}, bf16[2...) while((s32[]{:T(128)}, bf16[2,2,512,64]{2,3,1,0:T(8,128)(2,1)}, ...), condition=%wide.region_6.7_spmd, body=%wide.region_3.6_spmd.sunk | while | flops 279973888 | bytes 19304628 | solution.py:101
  264.4 2.1 fusion.238
  269.8 2.1 fusion.238
  278.3 3.4 fusion.137
  281.7 2.7 fusion.69
  290.2 34.2 %reduce-scatter.13.cloned.1.call-done = f32[256,512]{1,0:T(8,128)} async-done(((f32[1024,512]{1,0:T(8,128)}), f32[256,512]{1,0:T(8,128)}) %reduce-scatter.13.cloned.1.call-update) | async-done | bytes 524304 | tf_op jit(solution)/shard_map/reduce_scatter | solution.py:222
  327.4 30.8 %reduce-scatter.27.cloned.1.call-done = f32[256,512]{1,0:T(8,128)} async-done(((f32[1024,512]{1,0:T(8,128)}), f32[256,512]{1,0:T(8,128)}) %reduce-scatter.27.cloned.1.call-update) | async-done | bytes 524304 | tf_op jit(solution)/shard_map/reduce_scatter | solution.py:355
  358.2 2.1 multiply_reduce_fusion.1
  360.3 3.6 convert_reduce_fusion.6
  367.0 15.3 %all-gather.15.cloned.1.call-done = bf16[1024,512]{1,0:T(8,128)(2,1)} async-done(((bf16[256,512]{1,0:T(8,128)(2,1)}), bf16[1024,512]{1,0:T(8,128)(2,1)}) %all-gather.15.cloned.1.call-update) | async-done | bytes 1048592 | tf_op jit(solution)/shard_map/all_gather | solution.py:366
  382.3 2.4 convolution_convert_fusion
  388.2 16.5 %while.39 = (s32[]{:T(128)}, f32[2,1024,64]{1,2,0:T(8,128)}, f32[2,1024,64]{1,2,0:T(8,128)}, bf16[2,2,512,64]{2,3,1,0:T(8,128)(2,1)}, pred[2,512,1024]{2,1,0:T(8...) while((s32[]{:T(128)}, f32[2,1024,64]{1,2,0:T(8,128)}, ...), condition=%wide.region_29.30_spmd.clone, body=%wide.region_27.29_spmd.clone.sunk | while | flops 687602688 | bytes 50229632 | solution.py:148
  410.2 2.8 fusion.68
  413.0 2.8 convert_element_type.273
  415.9 4.2 all-gather.7.cloned.1.call-done
  420.1 4.1 fusion.70
  425.1 2.7 fusion.106
  428.1 3.4 fusion.146
  442.7 22.2 %all-reduce.1 = (f32[128]{0:T(128)}, f32[128]{0:T(128)}, f32[512]{0:T(512)}, f32[512]{0:T(512)}, f32[512]{0:T(512)}) all-reduce(f32[128]{0:T(128)S(1)} %reduce_sum.253, f32[128]{0:T(128)S(1)} %reduce_sum.255, f32[512]{0:T(512)S(1)} %copy-done.69, f32[512]{0:T(512)S(1)} %convert_reduce_fusion.1, ...), channel_id=1, replica_groups=mesh['dp'=8,'tensor'=4] {'dp'}, use_global_device_ids=true, to_apply=%region_39.40 | all-reduce | flops 1792 | bytes 14336 | tf_op jit(solution)/shard_map/psum | solution.py:414
  466.3 37.4 %all-reduce = (f32[512]{0:T(512)}, f32[512]{0:T(512)}, f32[512]{0:T(512)}, f32[512]{0:T(512)}, f32[512]{0:T(512)}, /*index=5*/f32[512]{0:T(512)}) all-reduce(f32[512]{0:T(512)S(1)} %get-tuple-element.250, f32[512]{0:T(512)S(1)} %get-tuple-element.254, f32[512]{0:T(512)S(1)} %copy-done.64, ...), channel_id=1, replica_groups=mesh['dp'=8,'tensor'=4] {'dp','tensor'}, use_global_device_ids=true, to_apply=%region_34.35 | all-reduce | flops 3072 | bytes 24576 | tf_op jit(solution)/shard_map/psum | solution.py:394
  503.7 2.0 fusion.93
  505.7 10.7 %reduce-scatter.15.cloned.1.call-done = f32[256,512]{1,0:T(8,128)} async-done(((f32[1024,512]{1,0:T(8,128)}), f32[256,512]{1,0:T(8,128)}) %reduce-scatter.15.cloned.1.call-update) | async-done | bytes 524304 | tf_op jit(solution)/shard_map/reduce_scatter | solution.py:237
  516.3 2.1 add_convert_fusion.1
  518.4 150.1 %all-reduce.5.cloned.1.call-done = (f32[512,128]{1,0:T(8,128)}, f32[512,128]{1,0:T(8,128)}, f32[512,128]{1,0:T(8,128)}, f32[128,512]{1,0:T(8,128)}, f32[128,512]...) async-done(((f32[512,128]{1,0:T(8,128)}, f32[512,128]{1,0:T(8,128)}, f32[512,128]{1,0:T(8,128)}, f32[128,512]{1,0:T(8,128)}, ...) | async-done | bytes 3670032 | tf_op jit(solution)/shard_map/psum | solution.py:414
  (362 shorter events, 126.1 us)
Async XLA Ops:
  7.2 177.9 %copy-start = (bf16[512,512]{1,0:T(8,128)(2,1)S(1)}, bf16[512,512]{1,0:T(8,128)(2,1)}, u32[]{:S(2)}) copy-start(bf16[512,512]{1,0:T(8,128)(2,1)} %param.45) | copy-start | bytes 1572868
  7.2 16.5 %copy-start.71 = (bf16[128]{0:T(256)(128)(2,1)S(1)}, bf16[128]{0:T(256)(128)(2,1)}, u32[]{:S(2)}) copy-start(bf16[128]{0:T(256)(128)(2,1)} %param.36) | copy-start | bytes 772
  7.2 16.5 %copy-start.70 = (bf16[128]{0:T(256)(128)(2,1)S(1)}, bf16[128]{0:T(256)(128)(2,1)}, u32[]{:S(2)}) copy-start(bf16[128]{0:T(256)(128)(2,1)} %param.33) | copy-start | bytes 772
  7.2 8.6 %copy-start.55 = (s32[1,1024]{1,0:T(1,128)S(1)}, s32[1,1024]{1,0:T(1,128)}, u32[]{:S(2)}) copy-start(s32[1,1024]{1,0:T(1,128)} %param.29) | copy-start | bytes 12292
  7.2 69.8 %reduce-scatter.21.cloned.1.call-start = ((), (), s32[]{:S(2)}) async-start(), calls=%async_computation.16 | async-start | bytes 2621440 | tf_op jit(solution)/shard_map/reduce_scatter | solution.py:222
  8.4 14.0 %copy-start.48 = (f32[256]{0:T(256)}, f32[256]{0:T(256)S(1)}, u32[]{:S(2)}) copy-start(f32[256]{0:T(256)S(1)} %broadcast_multiply_fusion.5) | copy-start | bytes 3076
  9.6 12.8 %copy-start.53 = (f32[256]{0:T(256)}, f32[256]{0:T(256)S(1)}, u32[]{:S(2)}) copy-start(f32[256]{0:T(256)S(1)} %add_rsqrt_fusion.1) | copy-start | bytes 3076
  11.0 15.6 %copy-start.23 = (bf16[512,128]{1,0:T(8,128)(2,1)S(1)}, bf16[512,128]{1,0:T(8,128)(2,1)}, u32[]{:S(2)}) copy-start(bf16[512,128]{1,0:T(8,128)(2,1)} %param.32) | copy-start | bytes 393220
  12.9 6.8 collective-permute-start.3
  13.4 10.4 %collective-permute-start.4 = (bf16[256,512]{1,0:T(8,128)(2,1)}, bf16[256,512]{1,0:T(8,128)(2,1)S(1)}, u32[]{:S(2)}, u32[]{:S(2)}) collective-permute-start(bf16[256,512]{1,0:T(8,128)(2,1)} %get-tuple-element.332), channel_id=1, source_target_pairs={{0,3},{1,0},{2,1},{3,2},{4,7},{5,4},{6,5},{7,6},{8,11},{9,8},{10,9... | collective-permute-start | bytes 786440 | tf_op jit(solution)/shard_map/ppermute | solution.py:181
  19.7 5.9 collective-permute-start.5
  29.0 10.7 %copy-start.22 = (bf16[128,512]{1,0:T(8,128)(2,1)S(1)}, bf16[128,512]{1,0:T(8,128)(2,1)}, u32[]{:S(2)}) copy-start(bf16[128,512]{1,0:T(8,128)(2,1)} %param.37) | copy-start | bytes 393220
  37.7 3.9 copy-start.5
  41.6 69.6 %reduce-scatter.19.cloned.1.call-start = ((), (), s32[]{:S(2)}) async-start(), calls=%async_computation.15 | async-start | bytes 2621440 | tf_op jit(solution)/shard_map/reduce_scatter | solution.py:223
  41.7 69.5 %copy-start.1 = (bf16[256,512]{1,0:T(8,128)(2,1)S(1)}, bf16[256,512]{1,0:T(8,128)(2,1)}, u32[]{:S(2)}) copy-start(bf16[256,512]{1,0:T(8,128)(2,1)} %param.28) | copy-start | bytes 786436
  44.4 87.5 %all-gather.9.cloned.1.call-start = ((), (), s32[]{:S(2)}) async-start(), calls=%async_computation.17 | async-start | bytes 1310720 | tf_op jit(solution)/shard_map/all_gather | solution.py:231
  45.1 67.6 %copy-start.51 = (f32[512]{0:T(512)}, f32[512]{0:T(512)S(1)}, u32[]{:S(2)}) copy-start(f32[512]{0:T(512)S(1)} %convert_element_type.253) | copy-start | bytes 6148
  112.7 21.9 %copy-start.50 = (f32[256]{0:T(256)}, f32[256]{0:T(256)S(1)}, u32[]{:S(2)}) copy-start(f32[256]{0:T(256)S(1)} %broadcast_multiply_fusion.4) | copy-start | bytes 3076
  114.9 51.2 %reduce-scatter.23.cloned.1.call-start = ((), (), s32[]{:S(2)}) async-start(), calls=%async_computation.18 | async-start | bytes 2621440 | tf_op jit(solution)/shard_map/reduce_scatter | solution.py:237
  134.6 50.5 %all-gather.11.cloned.1.call-start = ((), (), s32[]{:S(2)}) async-start(), calls=%async_computation.19 | async-start | bytes 1310720 | tf_op jit(solution)/shard_map/all_gather | solution.py:340
  135.3 37.5 %copy-start.52 = (f32[512]{0:T(512)}, f32[512]{0:T(512)S(1)}, u32[]{:S(2)}) copy-start(f32[512]{0:T(512)S(1)} %convert_element_type.257) | copy-start | bytes 6148
  168.2 57.1 %reduce-scatter.25.cloned.1.call-start = ((), (), s32[]{:S(2)}) async-start(), calls=%async_computation.20 | async-start | bytes 2621440 | tf_op jit(solution)/shard_map/reduce_scatter | solution.py:236
  193.7 88.0 %all-gather.13.cloned.1.call-start = ((), (), s32[]{:S(2)}) async-start(), calls=%async_computation.21 | async-start | bytes 1310720 | tf_op jit(solution)/shard_map/all_gather | solution.py:341
  227.5 62.8 %reduce-scatter.11.cloned.1.call-start = ((), (), s32[]{:S(2)}) async-start(), calls=%async_computation.10 | async-start | bytes 2621440 | tf_op jit(solution)/shard_map/reduce_scatter | solution.py:223
  230.9 10.2 %collective-permute-start = (bf16[256,512]{1,0:T(8,128)(2,1)}, bf16[256,512]{1,0:T(8,128)(2,1)}, u32[]{:S(2)}, u32[]{:S(2)}) collective-permute-start(bf16[256,512]{1,0:T(8,128)(2,1)} %get-tuple-element.336), channel_id=1, source_target_pairs={{0,1},{1,2},{2,3},{3,0},{4,5},{5,6},{6,7},{7,4},{8,9},{9,10},{10,1... | collective-permute-start | bytes 786440 | tf_op jit(solution)/shard_map/ppermute | solution.py:176
  230.9 13.6 %collective-permute-start.1 = (bf16[256,512]{1,0:T(8,128)(2,1)}, bf16[256,512]{1,0:T(8,128)(2,1)}, u32[]{:S(2)}, u32[]{:S(2)}) collective-permute-start(bf16[256,512]{1,0:T(8,128)(2,1)} %get-tuple-element.336), channel_id=1, source_target_pairs={{0,3},{1,0},{2,1},{3,2},{4,7},{5,4},{6,5},{7,6},{8,11},{9,8},{10,9... | collective-permute-start | bytes 786440 | tf_op jit(solution)/shard_map/ppermute | solution.py:181
  241.1 7.2 %collective-permute-start.2 = (bf16[256,512]{1,0:T(8,128)(2,1)}, bf16[256,512]{1,0:T(8,128)(2,1)}, u32[]{:S(2)}, u32[]{:S(2)}) collective-permute-start(bf16[256,512]{1,0:T(8,128)(2,1)} %collective-permute-done), channel_id=1, source_target_pairs={{0,1},{1,2},{2,3},{3,0},{4,5},{5,6},{6,7},{7,4},{8,9},{9,10},{10,1... | collective-permute-start | bytes 786440 | tf_op jit(solution)/shard_map/ppermute | solution.py:176
  258.7 65.7 %reduce-scatter.13.cloned.1.call-start = ((), (), s32[]{:S(2)}) async-start(), calls=%async_computation.11 | async-start | bytes 2621440 | tf_op jit(solution)/shard_map/reduce_scatter | solution.py:222
  278.2 80.0 %reduce-scatter.27.cloned.1.call-start = ((), (), s32[]{:S(2)}) async-start(), calls=%async_computation.22 | async-start | bytes 2621440 | tf_op jit(solution)/shard_map/reduce_scatter | solution.py:355
  284.5 97.9 %all-gather.15.cloned.1.call-start = ((), (), s32[]{:S(2)}) async-start(), calls=%async_computation.23 | async-start | bytes 1310720 | tf_op jit(solution)/shard_map/all_gather | solution.py:366
  365.4 44.8 %all-gather.17.cloned.1.call-start = ((), (), s32[]{:S(2)}) async-start(), calls=%async_computation.24 | async-start | bytes 1310720 | tf_op jit(solution)/shard_map/all_gather | solution.py:367
  366.0 54.1 %all-gather.7.cloned.1.call-start = ((), (), s32[]{:S(2)}) async-start(), calls=%async_computation.12 | async-start | bytes 1310720 | tf_op jit(solution)/shard_map/all_gather | solution.py:231
  366.8 98.2 %reduce-scatter.29.cloned.1.call-start = ((), (), s32[]{:S(2)}) async-start(), calls=%async_computation.25 | async-start | bytes 1310720 | tf_op jit(solution)/shard_map/reduce_scatter | solution.py:387
  413.0 7.1 %copy-start.21 = (bf16[512,512]{1,0:T(8,128)(2,1)S(1)}, bf16[512,512]{1,0:T(8,128)(2,1)}, u32[]{:S(2)}) copy-start(bf16[512,512]{1,0:T(8,128)(2,1)} %param.43) | copy-start | bytes 1572868
  415.8 89.9 %reduce-scatter.17.cloned.1.call-start = ((), (), s32[]{:S(2)}) async-start(), calls=%async_computation.14 | async-start | bytes 2621440 | tf_op jit(solution)/shard_map/reduce_scatter | solution.py:236
  424.2 92.1 %reduce-scatter.15.cloned.1.call-start = ((), (), s32[]{:S(2)}) async-start(), calls=%async_computation.13 | async-start | bytes 2621440 | tf_op jit(solution)/shard_map/reduce_scatter | solution.py:237
  427.8 240.7 %all-reduce.5.cloned.1.call-start = ((), (), s32[]{:S(2)}) async-start(), calls=%async_computation.26 | async-start | bytes 7340032 | tf_op jit(solution)/shard_map/psum | solution.py:414
  440.6 24.4 %copy-start.49 = (f32[256]{0:T(256)S(1)}, f32[256]{0:T(256)}, u32[]{:S(2)}) copy-start(f32[256]{0:T(256)} %copy-done.48) | copy-start | bytes 3076
  440.6 24.4 %copy-start.54 = (f32[256]{0:T(256)S(1)}, f32[256]{0:T(256)}, u32[]{:S(2)}) copy-start(f32[256]{0:T(256)} %copy-done.53) | copy-start | bytes 3076
  440.6 25.7 %copy-start.61 = (f32[512]{0:T(512)S(1)}, f32[512]{0:T(512)}, u32[]{:S(2)}) copy-start(f32[512]{0:T(512)} %get-tuple-element.247) | copy-start | bytes 6148
  440.6 25.7 %copy-start.62 = (f32[512]{0:T(512)S(1)}, f32[512]{0:T(512)}, u32[]{:S(2)}) copy-start(f32[512]{0:T(512)} %get-tuple-element.252) | copy-start | bytes 6148
  440.6 25.7 %copy-start.63 = (f32[512]{0:T(512)S(1)}, f32[512]{0:T(512)}, u32[]{:S(2)}) copy-start(f32[512]{0:T(512)} %get-tuple-element.324) | copy-start | bytes 6148
  440.6 25.7 %copy-start.64 = (f32[512]{0:T(512)S(1)}, f32[512]{0:T(512)}, u32[]{:S(2)}) copy-start(f32[512]{0:T(512)} %get-tuple-element.327) | copy-start | bytes 6148
  440.7 63.0 %copy-start.12 = (f32[256,512]{1,0:T(8,128)S(1)}, f32[256,512]{1,0:T(8,128)}, u32[]{:S(2)}) copy-start(f32[256,512]{1,0:T(8,128)} %copy-done.11) | copy-start | bytes 1572868
  440.7 75.6 %copy-start.9 = (f32[256,512]{1,0:T(8,128)S(1)}, f32[256,512]{1,0:T(8,128)}, u32[]{:S(2)}) copy-start(f32[256,512]{1,0:T(8,128)} %copy-done.8) | copy-start | bytes 1572868
  668.5 6.9 %copy-start.46 = (f32[128,512]{1,0:T(8,128)S(1)}, f32[128,512]{1,0:T(8,128)}, u32[]{:S(2)}) copy-start(f32[128,512]{1,0:T(8,128)} %get-tuple-element.592) | copy-start | bytes 786436
  668.5 7.6 %copy-start.34 = (f32[512,512]{1,0:T(8,128)S(1)}, f32[512,512]{1,0:T(8,128)}, u32[]{:S(2)}) copy-start(f32[512,512]{1,0:T(8,128)} %get-tuple-element.596) | copy-start | bytes 3145732
  670.3 6.8 copy-start.33
  (60 other events, 96.6 us)
Sparse Core Ops, SparseCore 0:
  41.7 35.3 reduce-scatter.20
  79.8 31.3 reduce-scatter.18
  115.1 16.7 all-gather.8
  134.7 31.4 reduce-scatter.22
  168.3 16.7 all-gather.10
  193.8 31.4 reduce-scatter.24
  227.6 19.7 all-gather.12
  258.8 31.4 reduce-scatter.10
  292.9 31.4 reduce-scatter.12
  326.8 31.4 reduce-scatter.26
  365.6 16.7 all-gather.14
  384.4 16.7 all-gather.16
  403.4 16.6 all-gather.6
  423.2 24.8 reduce-scatter.28
  450.5 32.1 reduce-scatter.16
  485.2 31.0 reduce-scatter.14
  522.6 145.9 all-reduce.4
